TPU v7x, 32 devices: a whole 2x2x4 slice. The times are simulated.
32 devices in a mesh: dom: 32 (over z, y, x, core).
Axes of the slice: x: 2, y: 2, z: 4, core: 2. Of those that a mesh axis runs over, the one named last changes fastest.
Arguments:
- elem_state: bfloat16 [1024, 5, 216], P('dom'), may hold values from -6 to 6
- mass_inverse: bfloat16 [1024, 216, 216], P('dom'), as said below
- jacobian: bfloat16 [1024, 216, 216], P('dom'), may hold values from -0.4375 to 0.4375
- elem_order: int32 [1024], P('dom'), may hold values from 2 to 5
- new_owner: int32 [1024], P('dom'), may hold values from 0 to 31, as said below
- neighbors: int32 [1024, 6], P('dom'), may hold values from -1 to 1023, as said below
- penalty: bfloat16 [1024, 6], P('dom'), may hold values from 0.049804688 to 0.5
- closure_in: bfloat16 [64, 5], replicated, may hold values from -2.5 to 2.5
- closure_out: bfloat16 [5, 64], replicated, may hold values from -0.75 to 0.75
Outputs:
- migrated: float32 [1536, 5, 216], P('dom')
- migrated_mass: bfloat16 [1536, 216, 216], P('dom')
- migrated_jacobian: bfloat16 [1536, 216, 216], P('dom')
Inputs may be any that keep to these rules, and one draw needn't show every extreme that they name: new_owner never falls along the elements; each element's new owner is the device that holds it before the repartition (32 elements a device, in order) or a device beside that one; at most 8 elements pass from one device to each neighbour, and each device owns between 16 and 48 elements afterwards; 8 and 48 are reached. `neighbors`: each entry is -1 or an element within 16 places of its own element along the curve; the distance 16 is reached. `mass_inverse`: each tile has a diagonal of order one and small off-diagonal entries.
All inputs are finite; a program needn't handle non-finite values.
Results may differ from a plain program's by a relative error of at most 0.01.
Values may be sent and summed in bfloat16 or wider, within the bound.
No kernel may reach another device: no remote copies, remote signals or barrier semaphores. Data moves between devices by JAX's collectives and lax.ppermute only.
A program may use at most 128 MiB of HBM per device.

v0:
```python
import jax
import jax.numpy as jnp
from jax import lax
from jax.sharding import PartitionSpec as P

SWEEPS = 2


def padded_2(shard, sides, width):
    for axis, dim in sides:
        size, length = (lax.axis_size(axis), shard.shape[dim])
        up = [(i, (i + 1) % size) for i in range(size - 1)]
        down = [(j, i) for i, j in up]
        last = lax.slice_in_dim(shard, length - width, length, axis=dim)
        initial = lax.slice_in_dim(shard, 0, width, axis=dim)
        before = lax.ppermute(last, axis, up)
        after = lax.ppermute(initial, axis, down)
        shard = jnp.concatenate([before, shard, after], axis=dim)
    return shard


def from_behind(shard, axis, by):
    size = lax.axis_size(axis)
    pairs = [(i, i + by) for i in range(size) if 0 <= i + by < size]
    return lax.ppermute(shard, axis, pairs)


def keep_mask(order_rows, node_count):
    limit = (order_rows + 1) ** 3
    node_ids = jnp.arange(node_count, dtype=jnp.int32)
    return (node_ids[None, :] < limit[:, None]).astype(jnp.float32)[:, None, :]


def run_sweeps(
    values,
    tiles_mass,
    tiles_jac,
    order_rows,
    near_index,
    weights_face,
    closure_in,
    closure_out,
    width,
):
    retained = keep_mask(order_rows, values.shape[2])
    weights_wide = weights_face.astype(jnp.float32)[:, :, None, None]
    current = values.astype(jnp.float32)
    for sweep_idx in range(SWEEPS):
        rounded = current.astype(jnp.bfloat16)
        weighted = jnp.einsum(
            "enm,evm->evn", tiles_mass, rounded, preferred_element_type=jnp.float32
        ).astype(jnp.bfloat16)
        extended = padded_2(weighted, (("dom", 0),), width)
        padded = jnp.concatenate(
            [extended, jnp.zeros((1,) + weighted.shape[1:], jnp.bfloat16)], axis=0
        )
        beside = jnp.take(padded, near_index, axis=0, mode="clip")
        difference = beside.astype(jnp.float32) - weighted.astype(jnp.float32)[:, None]
        coupling = jnp.sum(weights_wide * difference, axis=1)
        transport = jnp.einsum(
            "enm,evn->evm", tiles_jac, weighted, preferred_element_type=jnp.float32
        )
        hidden = jnp.tanh(
            jnp.einsum("hv,evn->ehn", closure_in, rounded, preferred_element_type=jnp.float32)
        ).astype(jnp.bfloat16)
        closure = jnp.einsum("vh,ehn->evn", closure_out, hidden, preferred_element_type=jnp.float32)
        current = (current + transport + coupling + closure) * retained
    return current


def claim(owners, position, devices, moving):
    row_count = owners.shape[0]
    row_ids = jnp.arange(row_count, dtype=jnp.int32)
    owned = owners == position
    owned = owned & ((row_ids >= moving) | (position > 0))
    owned = owned & ((row_ids < row_count - moving) | (position < devices - 1))
    owned_ints = owned.astype(jnp.int32)
    leading = jnp.argmax(owned_ints)
    filled = jnp.sum(owned_ints)
    return (leading, filled)


def place(values, leading, filled):
    padded = jnp.concatenate([values, jnp.zeros_like(values)], axis=0)
    window = lax.dynamic_slice_in_dim(padded, leading, values.shape[0], 0)
    slot_ids = jnp.arange(values.shape[0], dtype=jnp.int32)
    live = (slot_ids < filled).reshape((values.shape[0],) + (1,) * (values.ndim - 1))
    return jnp.where(live, window, jnp.zeros((), values.dtype))


def neighbor_index(adjacent, position, local_count, width):
    core_anchor = position * local_count - width
    span = local_count + 2 * width
    located = jnp.clip(adjacent - core_anchor, 0, span - 1)
    return jnp.where(adjacent < 0, span, located)


def shards(
    elem_state,
    mass_inverse,
    jacobian,
    elem_order,
    new_owner,
    neighbors,
    penalty,
    closure_in,
    closure_out,
):
    local_count = elem_state.shape[0]
    moving = local_count // 4
    reach = local_count // 2
    position = lax.axis_index("dom")
    devices = lax.axis_size("dom")

    def ship_tiles(start_row, offset):
        return from_behind(
            (
                mass_inverse[start_row : start_row + moving],
                jacobian[start_row : start_row + moving],
            ),
            "dom",
            offset,
        )

    tiles_left = ship_tiles(local_count - moving, 1)
    tiles_right = ship_tiles(0, -1)
    near_index = neighbor_index(neighbors, position, local_count, reach)
    current = run_sweeps(
        elem_state,
        mass_inverse,
        jacobian,
        elem_order,
        near_index,
        penalty,
        closure_in,
        closure_out,
        reach,
    )

    def ship_state(start_row, offset):
        return from_behind(
            current[start_row : start_row + moving].astype(jnp.bfloat16), "dom", offset
        ).astype(jnp.float32)

    def ship_owner(start_row, offset):
        return from_behind(new_owner[start_row : start_row + moving], "dom", offset)

    joined = jnp.concatenate(
        [ship_state(local_count - moving, 1), current, ship_state(0, -1)], axis=0
    )
    owners = jnp.concatenate(
        [ship_owner(local_count - moving, 1), new_owner, ship_owner(0, -1)], axis=0
    )
    joined_mass = jnp.concatenate([tiles_left[0], mass_inverse, tiles_right[0]], axis=0)
    joined_jac = jnp.concatenate([tiles_left[1], jacobian, tiles_right[1]], axis=0)
    leading, filled = claim(owners, position, devices, moving)
    return (
        place(joined, leading, filled),
        place(joined_mass, leading, filled),
        place(joined_jac, leading, filled),
    )


def solution(mesh):
    placed = (
        P("dom", None, None),
        P("dom", None, None),
        P("dom", None, None),
        P("dom"),
        P("dom"),
        P("dom", None),
        P("dom", None),
        P(),
        P(),
    )
    return jax.shard_map(
        shards,
        mesh=mesh,
        in_specs=placed,
        out_specs=(P("dom", None, None), P("dom", None, None), P("dom", None, None)),
        check_vma=False,
    )
```

profile of v0, /device:TPU:7, one launch (start us, length us, event | category | flops | bytes accessed | tf_op | source)
XLA Modules:
  0.0 104.0 jit_solution(15856952869262884062)
XLA Ops:
  0.7 1.5 %fusion.45 = (s32[8]{0:T(128)}, s32[8]{0:T(128)}) fusion(s32[32]{0:T(128)} %param.13), kind=kLoop, calls=%fused_computation.73 | loop fusion | bytes 128 | tf_op jit(solution)/shard_map/slice | solution.py:146
  2.1 3.7 %collective-permute-start = (s32[8]{0:T(128)}, s32[8]{0:T(128)}, u32[]{:S(2)}, u32[]{:S(2)}) collective-permute-start(s32[8]{0:T(128)} %get-tuple-element.23), channel_id=1, source_target_pairs={{0,1},{1,2},{2,3},{3,4},{4,5},{5,6},{6,7},{7,8},{8,9},{9,10},{10,1... | collective-permute-start | bytes 104 | tf_op jit(solution)/shard_map/ppermute | solution.py:25
  5.8 2.2 %collective-permute-start.1 = (s32[8]{0:T(128)}, s32[8]{0:T(128)}, u32[]{:S(2)}, u32[]{:S(2)}) collective-permute-start(s32[8]{0:T(128)} %get-tuple-element.24), channel_id=1, source_target_pairs={{1,0},{2,1},{3,2},{4,3},{5,4},{6,5},{7,6},{8,7},{9,8},{10,9},{11,1... | collective-permute-start | bytes 104 | tf_op jit(solution)/shard_map/ppermute | solution.py:25
  8.0 3.8 %fusion.46 = (f32[32,5,216]{2,1,0:T(8,128)}, bf16[32,5,216]{2,1,0:T(8,128)(2,1)S(1)}) fusion(bf16[32,216,216]{2,1,0:T(8,128)(2,1)} %param.10, bf16[32,5,216]{2,0,1:T(8,128)(2,1)} %param.9), kind=kOutput, calls=%fused_computation.74 | convolution fusion | flops 14999040 | bytes 3262464 | tf_op jit(solution)/shard_map/enm,evm->evn/dot_general | solution.py:50
  12.5 5.4 %collective-permute-start.2 = (bf16[16,5,216]{2,1,0:T(8,128)(2,1)}, bf16[16,5,216]{2,1,0:T(8,128)(2,1)}, u32[]{:S(2)}, u32[]{:S(2)}) collective-permute-start(bf16[16,5,216]{2,1,0:T(8,128)(2,1)} %get-tuple-element.19), channel_id=1, source_target_pairs={{0,1},{1,2},{2,3},{3,4},{4,5},{5,6},{6,7},{7,8},{8,9},{9,10},{10,1... | collective-permute-start | bytes 103688 | tf_op jit(solution)/shard_map/ppermute | solution.py:16
  18.0 1.9 %collective-permute-start.3 = (bf16[16,5,216]{2,1,0:T(8,128)(2,1)}, bf16[16,5,216]{2,1,0:T(8,128)(2,1)}, u32[]{:S(2)}, u32[]{:S(2)}) collective-permute-start(bf16[16,5,216]{2,1,0:T(8,128)(2,1)} %get-tuple-element.20), channel_id=1, source_target_pairs={{1,0},{2,1},{3,2},{4,3},{5,4},{6,5},{7,6},{8,7},{9,8},{10,9},{11,1... | collective-permute-start | bytes 103688 | tf_op jit(solution)/shard_map/ppermute | solution.py:17
  19.9 1.4 %fusion.41 = (bf16[8,216,216]{2,1,0:T(8,128)(2,1)}, bf16[8,216,216]{2,1,0:T(8,128)(2,1)}) fusion(bf16[32,216,216]{2,1,0:T(8,128)(2,1)S(1)} %copy-done.1), kind=kLoop, calls=%fused_computation.69 | loop fusion | bytes 2985984 | tf_op jit(solution)/shard_map/slice | solution.py:118
  21.3 1.9 %collective-permute-start.9 = (bf16[8,216,216]{2,1,0:T(8,128)(2,1)}, bf16[8,216,216]{2,1,0:T(8,128)(2,1)}, u32[]{:S(2)}, u32[]{:S(2)}) collective-permute-start(bf16[8,216,216]{2,1,0:T(8,128)(2,1)} %get-tuple-element.15), channel_id=1, source_target_pairs={{1,0},{2,1},{3,2},{4,3},{5,4},{6,5},{7,6},{8,7},{9,8},{10,9},{11,1... | collective-permute-start | bytes 2239496 | tf_op jit(solution)/shard_map/ppermute | solution.py:25
  23.2 1.3 %fusion.48 = f32[32,5,216]{2,1,0:T(8,128)} fusion(bf16[32,5,216]{2,1,0:T(8,128)(2,1)S(1)} %get-tuple-element.26, bf16[32,216,216]{2,1,0:T(8,128)(2,1)S(1)} %copy-done.2), kind=kOutput, calls=%fused_computation.76 | convolution fusion | flops 14929920 | bytes 3193344 | tf_op jit(solution)/shard_map/enm,evn->evm/dot_general | solution.py:60
  27.9 1.4 %copy.37 = f32[32,6]{1,0:T(8,128)} copy(bf16[32,6]{0,1:T(8,128)(2,1)} %param.15) | data formatting | bytes 1152 | tf_op jit(solution)/shard_map/convert_element_type | solution.py:46
  30.6 2.2 %fusion.15 = f32[32,216,5]{1,2,0:T(8,128)} fusion(bf16[32,5,216]{2,0,1:T(8,128)(2,1)} %param.9, bf16[5,64]{1,0:T(8,128)(2,1)S(1)} %copy-done, bf16[64,5]{0,1:T(8,128)(2,1)} %param.16), kind=kOutput, calls=%fused_computation.28 | convolution fusion | flops 9289728 | bytes 208640 | tf_op jit(solution)/shard_map/vh,ehn->evn/dot_general | solution.py:66
  32.8 5.4 %collective-permute-start.8 = (bf16[8,216,216]{2,1,0:T(8,128)(2,1)}, bf16[8,216,216]{2,1,0:T(8,128)(2,1)}, u32[]{:S(2)}, u32[]{:S(2)}) collective-permute-start(bf16[8,216,216]{2,1,0:T(8,128)(2,1)} %get-tuple-element.16), channel_id=1, source_target_pairs={{0,1},{1,2},{2,3},{3,4},{4,5},{5,6},{6,7},{7,8},{8,9},{9,10},{10,1... | collective-permute-start | bytes 2239496 | tf_op jit(solution)/shard_map/ppermute | solution.py:25
  38.3 1.9 %collective-permute-start.11 = (bf16[8,216,216]{2,1,0:T(8,128)(2,1)}, bf16[8,216,216]{2,1,0:T(8,128)(2,1)}, u32[]{:S(2)}, u32[]{:S(2)}) collective-permute-start(bf16[8,216,216]{2,1,0:T(8,128)(2,1)} %get-tuple-element.13), channel_id=1, source_target_pairs={{1,0},{2,1},{3,2},{4,3},{5,4},{6,5},{7,6},{8,7},{9,8},{10,9},{11,1... | collective-permute-start | bytes 2239496 | tf_op jit(solution)/shard_map/ppermute | solution.py:25
  40.2 2.0 %fusion.35 = (s32[]{:T(128)}, s32[48]{0:T(128)}) fusion(pred[]{:T(512)S(6)} %lt.55, pred[]{:T(512)S(6)} %gt.5, s32[]{:T(128)S(6)} %axis_index.12, s32[8]{0:T(128)} %collective-permute-done.1, s32[32]{0:T(128)S(1)} %copy-done.9, s32[8]{0:T(128)} %collective-permute-done), kind=kLoop, calls=%fused_computation.65 | loop fusion | flops 527 | bytes 394 | tf_op jit(solution)/shard_map/reduce_sum | solution.py:79
  42.2 1.8 %maximum_maximum_fusion = bf16[65,5,216]{2,1,0:T(8,128)(2,1)} fusion(bf16[16,5,216]{2,1,0:T(8,128)(2,1)} %collective-permute-done.3, bf16[32,5,216]{2,1,0:T(8,128)(2,1)} %copy-done.5, bf16[16,5,216]{2,1,0:T(8,128)(2,1)} %collective-permute-done.2, bf16[65]{0:T(256)(128)(2,1)S(1)} %pad.19.clone), kind=kLoop, calls=%fused_computation.35 | loop fusion | flops 210600 | bytes 278770 | tf_op jit(solution)/shard_map/concatenate | solution.py:54
  44.0 2.7 %gather_fusion = bf16[192,5,216]{2,1,0:T(8,128)(2,1)} fusion(bf16[65,5,216]{2,1,0:T(8,128)(2,1)} %maximum_maximum_fusion, s32[1024]{0:T(1024)S(1)} %pad_clamp_fusion), kind=kCustom, calls=%fused_computation | custom fusion | bytes 830208 | tf_op jit(solution)/shard_map/jit(_take)/gather | solution.py:57
  46.7 1.8 %fusion.11 = f32[32,5,216]{2,1,0:T(8,128)S(1)} fusion(bf16[32,6,5,216]{3,2,1,0:T(8,128)(2,1)} %bitcast.42, f32[32,5,216]{2,1,0:T(8,128)} %get-tuple-element.25, f32[32,6]{1,0:T(8,128)} %copy.37), kind=kLoop, calls=%fused_computation.24 | loop fusion | flops 794880 | bytes 691968 | tf_op jit(solution)/shard_map/reduce_sum | solution.py:59
  48.5 2.0 %fusion.38 = (bf16[32,5,216]{2,0,1:T(8,128)(2,1)S(1)}, f32[32,5,216]{2,0,1:T(8,128)}) fusion(f32[32,216]{1,0:T(8,128)} %fusion.28, f32[32,216,5]{1,2,0:T(8,128)} %fusion.15, f32[32,5,216]{2,1,0:T(8,128)S(1)} %fusion.11, f32[32,5,216]{2,1,0:T(8,128)} %fusion.48, bf16[32,5,216]{2,0,1:T(8,128)(2,1)} %param.9), kind=kLoop, calls=%fused_computation.67 | loop fusion | flops 207360 | bytes 718848 | tf_op jit(solution)/shard_map/convert_element_type | solution.py:49
  50.4 1.8 %fusion.47 = (f32[32,5,216]{2,1,0:T(8,128)}, bf16[32,5,216]{2,1,0:T(8,128)(2,1)S(1)}) fusion(bf16[32,216,216]{2,1,0:T(8,128)(2,1)S(1)} %copy-done.1, bf16[32,5,216]{2,0,1:T(8,128)(2,1)S(1)} %get-tuple-element.9), kind=kOutput, calls=%fused_computation.75 | convolution fusion | flops 14999040 | bytes 3262464 | tf_op jit(solution)/shard_map/enm,evm->evn/dot_general | solution.py:50
  54.2 5.6 %collective-permute-start.4 = (bf16[16,5,216]{2,1,0:T(8,128)(2,1)}, bf16[16,5,216]{2,1,0:T(8,128)(2,1)}, u32[]{:S(2)}, u32[]{:S(2)}) collective-permute-start(bf16[16,5,216]{2,1,0:T(8,128)(2,1)} %get-tuple-element.17), channel_id=1, source_target_pairs={{0,1},{1,2},{2,3},{3,4},{4,5},{5,6},{6,7},{7,8},{8,9},{9,10},{10,1... | collective-permute-start | bytes 103688 | tf_op jit(solution)/shard_map/ppermute | solution.py:16
  59.8 1.9 %collective-permute-start.5 = (bf16[16,5,216]{2,1,0:T(8,128)(2,1)}, bf16[16,5,216]{2,1,0:T(8,128)(2,1)}, u32[]{:S(2)}, u32[]{:S(2)}) collective-permute-start(bf16[16,5,216]{2,1,0:T(8,128)(2,1)} %get-tuple-element.18), channel_id=1, source_target_pairs={{1,0},{2,1},{3,2},{4,3},{5,4},{6,5},{7,6},{8,7},{9,8},{10,9},{11,1... | collective-permute-start | bytes 103688 | tf_op jit(solution)/shard_map/ppermute | solution.py:17
  61.7 2.2 %fusion.14 = f32[32,216,5]{1,2,0:T(8,128)} fusion(bf16[32,5,216]{2,0,1:T(8,128)(2,1)} %copy-done.7, bf16[5,64]{1,0:T(8,128)(2,1)S(1)} %copy-done, bf16[64,5]{0,1:T(8,128)(2,1)} %param.16), kind=kOutput, calls=%fused_computation.27 | convolution fusion | flops 9289728 | bytes 208640 | tf_op jit(solution)/shard_map/vh,ehn->evn/dot_general | solution.py:66
  63.9 5.4 %collective-permute-start.10 = (bf16[8,216,216]{2,1,0:T(8,128)(2,1)}, bf16[8,216,216]{2,1,0:T(8,128)(2,1)}, u32[]{:S(2)}, u32[]{:S(2)}) collective-permute-start(bf16[8,216,216]{2,1,0:T(8,128)(2,1)} %get-tuple-element.14), channel_id=1, source_target_pairs={{0,1},{1,2},{2,3},{3,4},{4,5},{5,6},{6,7},{7,8},{8,9},{9,10},{10,1... | collective-permute-start | bytes 2239496 | tf_op jit(solution)/shard_map/ppermute | solution.py:25
  69.4 1.8 %maximum_maximum_fusion.1 = bf16[65,5,216]{2,1,0:T(8,128)(2,1)} fusion(bf16[16,5,216]{2,1,0:T(8,128)(2,1)} %collective-permute-done.5, bf16[32,5,216]{2,1,0:T(8,128)(2,1)} %copy-done.6, bf16[16,5,216]{2,1,0:T(8,128)(2,1)} %collective-permute-done.4, bf16[65]{0:T(256)(128)(2,1)S(1)} %pad.19.clone), kind=kLoop, calls=%fused_computation.36 | loop fusion | flops 210600 | bytes 278770 | tf_op jit(solution)/shard_map/concatenate | solution.py:54
  71.2 2.7 %gather_fusion.1 = bf16[192,5,216]{2,1,0:T(8,128)(2,1)} fusion(bf16[65,5,216]{2,1,0:T(8,128)(2,1)} %maximum_maximum_fusion.1, s32[1024]{0:T(1024)S(1)} %pad_clamp_fusion), kind=kCustom, calls=%fused_computation.1 | custom fusion | bytes 830208 | tf_op jit(solution)/shard_map/jit(_take)/gather | solution.py:57
  73.8 1.7 %fusion.9 = f32[32,5,216]{2,1,0:T(8,128)S(1)} fusion(bf16[32,6,5,216]{3,2,1,0:T(8,128)(2,1)} %bitcast.41, f32[32,5,216]{2,1,0:T(8,128)} %get-tuple-element.27, f32[32,6]{1,0:T(8,128)} %copy.37), kind=kLoop, calls=%fused_computation.21 | loop fusion | flops 794880 | bytes 691968 | tf_op jit(solution)/shard_map/reduce_sum | solution.py:59
  75.5 2.0 %fusion.36 = (bf16[32,5,216]{2,0,1:T(8,128)(2,1)S(1)}, f32[32,5,216]{2,0,1:T(8,128)}) fusion(f32[32,216]{1,0:T(8,128)} %fusion.28, f32[32,216,5]{1,2,0:T(8,128)} %fusion.14, f32[32,5,216]{2,1,0:T(8,128)S(1)} %fusion.9, f32[32,5,216]{2,0,1:T(8,128)} %get-tuple-element.10, f32[32,5,216]{2,1,0:T(8,128)} %fusion.49), kind=kLoop, calls=%fused_computation.66 | loop fusion | flops 172800 | bytes 787968 | tf_op jit(solution)/shard_map/convert.1
  78.2 1.9 %collective-permute-start.7 = (bf16[8,5,216]{2,0,1:T(8,128)(2,1)S(1)}, bf16[8,5,216]{2,0,1:T(8,128)(2,1)S(1)}, u32[]{:S(2)}, u32[]{:S(2)}) collective-permute-start(bf16[8,5,216]{2,0,1:T(8,128)(2,1)S(1)} %get-tuple-element.21), channel_id=1, source_target_pairs={{1,0},{2,1},{3,2},{4,3},{5,4},{6,5},{7,6},{8,7},{9,8},{10,9},{11,1... | collective-permute-start | bytes 51848 | tf_op jit(solution)/shard_map/ppermute | solution.py:25
  80.8 4.2 %collective-permute-done.7 = bf16[8,5,216]{2,0,1:T(8,128)(2,1)S(1)} collective-permute-done((bf16[8,5,216]{2,0,1:T(8,128)(2,1)S(1)}, bf16[8,5,216]{2,0,1:T(8,128)(2,1)S(1)}, u32[]{:S(2)}, u32[]{:S(2)}) %collective-permute-start.7) | collective-permute-done | bytes 17312 | tf_op jit(solution)/shard_map/ppermute | solution.py:25
  85.6 1.9 %collective-permute-start.6 = (bf16[8,5,216]{2,0,1:T(8,128)(2,1)}, bf16[8,5,216]{2,0,1:T(8,128)(2,1)}, u32[]{:S(2)}, u32[]{:S(2)}) collective-permute-start(bf16[8,5,216]{2,0,1:T(8,128)(2,1)} %get-tuple-element.22), channel_id=1, source_target_pairs={{0,1},{1,2},{2,3},{3,4},{4,5},{5,6},{6,7},{7,8},{8,9},{9,10},{10,1... | collective-permute-start | bytes 51848 | tf_op jit(solution)/shard_map/ppermute | solution.py:25
  92.0 1.8 %fusion.19 = f32[48,5,216]{2,0,1:T(8,128)} fusion(f32[48,5,216]{2,0,1:T(8,128)S(1)} %broadcast_in_dim.45, s32[]{:T(128)S(6)} %select_n.25, f32[8,5,216]{2,0,1:T(8,128)S(1)} %convert_element_type.73, f32[32,5,216]{2,0,1:T(8,128)} %get-tuple-element.8, f32[8,5,216]{2,0,1:T(8,128)S(1)} %convert_element_type.74, pred[48]{0:T(512)(128)(4,1)S(1)} %iota_compare_fusion.1), kind=kLoop, calls=%fused_computation.40 | loop fusion | flops 207360 | bytes 622132 | tf_op jit(solution)/shard_map/jit(_where)/select_n | solution.py:88
  94.1 9.9 %fusion.3 = (bf16[48,216,216]{2,1,0:T(8,128)(2,1)}, bf16[48,216,216]{2,1,0:T(8,128)(2,1)}) fusion(bf16[48,216,216]{2,1,0:T(8,128)(2,1)S(1)} %broadcast.23, s32[]{:T(128)S(6)} %select_n.25, bf16[8,216,216]{2,1,0:T(8,128)(2,1)} %collective-permute-done.10, bf16[32,216,216]{2,1,0:T(8,128)(2,1)S(1)} %copy-done.4, ...), kind=kLoop, calls=%fused_computation.12 | loop fusion | flops 17915904 | bytes 22394932 | tf_op jit(solution)/shard_map/jit(_where)/select_n | solution.py:88
  (55 shorter events, 12.2 us)
Async XLA Ops:
  0.6 30.0 %copy-start = (bf16[5,64]{1,0:T(8,128)(2,1)S(1)}, bf16[5,64]{1,0:T(8,128)(2,1)}, u32[]{:S(2)}) copy-start(bf16[5,64]{1,0:T(8,128)(2,1)} %param.17) | copy-start | bytes 1924
  0.6 19.2 %copy-start.1 = (bf16[32,216,216]{2,1,0:T(8,128)(2,1)S(1)}, bf16[32,216,216]{2,1,0:T(8,128)(2,1)}, u32[]{:S(2)}) copy-start(bf16[32,216,216]{2,1,0:T(8,128)(2,1)} %param.10) | copy-start | bytes 8957956
  2.1 30.7 %collective-permute-start = (s32[8]{0:T(128)}, s32[8]{0:T(128)}, u32[]{:S(2)}, u32[]{:S(2)}) collective-permute-start(s32[8]{0:T(128)} %get-tuple-element.23), channel_id=1, source_target_pairs={{0,1},{1,2},{2,3},{3,4},{4,5},{5,6},{6,7},{7,8},{8,9},{9,10},{10,1... | collective-permute-start | bytes 104 | tf_op jit(solution)/shard_map/ppermute | solution.py:25
  5.8 17.4 %copy-start.2 = (bf16[32,216,216]{2,1,0:T(8,128)(2,1)S(1)}, bf16[32,216,216]{2,1,0:T(8,128)(2,1)}, u32[]{:S(2)}) copy-start(bf16[32,216,216]{2,1,0:T(8,128)(2,1)} %param.11) | copy-start | bytes 8957956
  5.8 32.4 %collective-permute-start.1 = (s32[8]{0:T(128)}, s32[8]{0:T(128)}, u32[]{:S(2)}, u32[]{:S(2)}) collective-permute-start(s32[8]{0:T(128)} %get-tuple-element.24), channel_id=1, source_target_pairs={{1,0},{2,1},{3,2},{4,3},{5,4},{6,5},{7,6},{8,7},{9,8},{10,9},{11,1... | collective-permute-start | bytes 104 | tf_op jit(solution)/shard_map/ppermute | solution.py:25
  11.8 12.7 %copy-start.5 = (bf16[32,5,216]{2,1,0:T(8,128)(2,1)}, bf16[32,5,216]{2,1,0:T(8,128)(2,1)S(1)}, u32[]{:S(2)}) copy-start(bf16[32,5,216]{2,1,0:T(8,128)(2,1)S(1)} %get-tuple-element.26) | copy-start | bytes 207364
  12.5 29.7 %collective-permute-start.2 = (bf16[16,5,216]{2,1,0:T(8,128)(2,1)}, bf16[16,5,216]{2,1,0:T(8,128)(2,1)}, u32[]{:S(2)}, u32[]{:S(2)}) collective-permute-start(bf16[16,5,216]{2,1,0:T(8,128)(2,1)} %get-tuple-element.19), channel_id=1, source_target_pairs={{0,1},{1,2},{2,3},{3,4},{4,5},{5,6},{6,7},{7,8},{8,9},{9,10},{10,1... | collective-permute-start | bytes 103688 | tf_op jit(solution)/shard_map/ppermute | solution.py:16
  18.0 24.2 %collective-permute-start.3 = (bf16[16,5,216]{2,1,0:T(8,128)(2,1)}, bf16[16,5,216]{2,1,0:T(8,128)(2,1)}, u32[]{:S(2)}, u32[]{:S(2)}) collective-permute-start(bf16[16,5,216]{2,1,0:T(8,128)(2,1)} %get-tuple-element.20), channel_id=1, source_target_pairs={{1,0},{2,1},{3,2},{4,3},{5,4},{6,5},{7,6},{8,7},{9,8},{10,9},{11,1... | collective-permute-start | bytes 103688 | tf_op jit(solution)/shard_map/ppermute | solution.py:17
  21.3 72.5 %collective-permute-start.9 = (bf16[8,216,216]{2,1,0:T(8,128)(2,1)}, bf16[8,216,216]{2,1,0:T(8,128)(2,1)}, u32[]{:S(2)}, u32[]{:S(2)}) collective-permute-start(bf16[8,216,216]{2,1,0:T(8,128)(2,1)} %get-tuple-element.15), channel_id=1, source_target_pairs={{1,0},{2,1},{3,2},{4,3},{5,4},{6,5},{7,6},{8,7},{9,8},{10,9},{11,1... | collective-permute-start | bytes 2239496 | tf_op jit(solution)/shard_map/ppermute | solution.py:25
  23.2 2.7 %copy-start.12 = (s32[32]{0:T(128)S(1)}, s32[32]{0:T(128)}, u32[]{:S(2)}) copy-start(s32[32]{0:T(128)} %param.12) | copy-start | bytes 388
  23.2 3.2 %copy-start.10 = (s32[32,6]{0,1:T(8,128)S(1)}, s32[32,6]{0,1:T(8,128)}, u32[]{:S(2)}) copy-start(s32[32,6]{0,1:T(8,128)} %param.14) | copy-start | bytes 2308
  23.2 17.0 %copy-start.9 = (s32[32]{0:T(128)S(1)}, s32[32]{0:T(128)}, u32[]{:S(2)}) copy-start(s32[32]{0:T(128)} %param.13) | copy-start | bytes 388
  32.8 61.0 %collective-permute-start.8 = (bf16[8,216,216]{2,1,0:T(8,128)(2,1)}, bf16[8,216,216]{2,1,0:T(8,128)(2,1)}, u32[]{:S(2)}, u32[]{:S(2)}) collective-permute-start(bf16[8,216,216]{2,1,0:T(8,128)(2,1)} %get-tuple-element.16), channel_id=1, source_target_pairs={{0,1},{1,2},{2,3},{3,4},{4,5},{5,6},{6,7},{7,8},{8,9},{9,10},{10,1... | collective-permute-start | bytes 2239496 | tf_op jit(solution)/shard_map/ppermute | solution.py:25
  38.3 55.5 %collective-permute-start.11 = (bf16[8,216,216]{2,1,0:T(8,128)(2,1)}, bf16[8,216,216]{2,1,0:T(8,128)(2,1)}, u32[]{:S(2)}, u32[]{:S(2)}) collective-permute-start(bf16[8,216,216]{2,1,0:T(8,128)(2,1)} %get-tuple-element.13), channel_id=1, source_target_pairs={{1,0},{2,1},{3,2},{4,3},{5,4},{6,5},{7,6},{8,7},{9,8},{10,9},{11,1... | collective-permute-start | bytes 2239496 | tf_op jit(solution)/shard_map/ppermute | solution.py:25
  46.6 6.3 %copy-start.3 = (bf16[32,216,216]{2,1,0:T(8,128)(2,1)S(1)}, bf16[32,216,216]{2,1,0:T(8,128)(2,1)}, u32[]{:S(2)}) copy-start(bf16[32,216,216]{2,1,0:T(8,128)(2,1)} %param.11) | copy-start | bytes 8957956
  50.4 3.8 %copy-start.7 = (bf16[32,5,216]{2,0,1:T(8,128)(2,1)}, bf16[32,5,216]{2,0,1:T(8,128)(2,1)S(1)}, u32[]{:S(2)}) copy-start(bf16[32,5,216]{2,0,1:T(8,128)(2,1)S(1)} %get-tuple-element.9) | copy-start | bytes 207364
  52.2 2.0 %copy-start.6 = (bf16[32,5,216]{2,1,0:T(8,128)(2,1)}, bf16[32,5,216]{2,1,0:T(8,128)(2,1)S(1)}, u32[]{:S(2)}) copy-start(bf16[32,5,216]{2,1,0:T(8,128)(2,1)S(1)} %get-tuple-element.28) | copy-start | bytes 207364
  54.2 25.9 %copy-start.11 = (s32[48]{0:T(128)S(1)}, s32[48]{0:T(128)}, u32[]{:S(2)}) copy-start(s32[48]{0:T(128)} %get-tuple-element.6) | copy-start | bytes 580
  54.2 9.7 %collective-permute-start.4 = (bf16[16,5,216]{2,1,0:T(8,128)(2,1)}, bf16[16,5,216]{2,1,0:T(8,128)(2,1)}, u32[]{:S(2)}, u32[]{:S(2)}) collective-permute-start(bf16[16,5,216]{2,1,0:T(8,128)(2,1)} %get-tuple-element.17), channel_id=1, source_target_pairs={{0,1},{1,2},{2,3},{3,4},{4,5},{5,6},{6,7},{7,8},{8,9},{9,10},{10,1... | collective-permute-start | bytes 103688 | tf_op jit(solution)/shard_map/ppermute | solution.py:16
  59.8 9.6 %collective-permute-start.5 = (bf16[16,5,216]{2,1,0:T(8,128)(2,1)}, bf16[16,5,216]{2,1,0:T(8,128)(2,1)}, u32[]{:S(2)}, u32[]{:S(2)}) collective-permute-start(bf16[16,5,216]{2,1,0:T(8,128)(2,1)} %get-tuple-element.18), channel_id=1, source_target_pairs={{1,0},{2,1},{3,2},{4,3},{5,4},{6,5},{7,6},{8,7},{9,8},{10,9},{11,1... | collective-permute-start | bytes 103688 | tf_op jit(solution)/shard_map/ppermute | solution.py:17
  63.9 29.8 %collective-permute-start.10 = (bf16[8,216,216]{2,1,0:T(8,128)(2,1)}, bf16[8,216,216]{2,1,0:T(8,128)(2,1)}, u32[]{:S(2)}, u32[]{:S(2)}) collective-permute-start(bf16[8,216,216]{2,1,0:T(8,128)(2,1)} %get-tuple-element.14), channel_id=1, source_target_pairs={{0,1},{1,2},{2,3},{3,4},{4,5},{5,6},{6,7},{7,8},{8,9},{9,10},{10,1... | collective-permute-start | bytes 2239496 | tf_op jit(solution)/shard_map/ppermute | solution.py:25
  78.2 6.9 %collective-permute-start.7 = (bf16[8,5,216]{2,0,1:T(8,128)(2,1)S(1)}, bf16[8,5,216]{2,0,1:T(8,128)(2,1)S(1)}, u32[]{:S(2)}, u32[]{:S(2)}) collective-permute-start(bf16[8,5,216]{2,0,1:T(8,128)(2,1)S(1)} %get-tuple-element.21), channel_id=1, source_target_pairs={{1,0},{2,1},{3,2},{4,3},{5,4},{6,5},{7,6},{8,7},{9,8},{10,9},{11,1... | collective-permute-start | bytes 51848 | tf_op jit(solution)/shard_map/ppermute | solution.py:25
  85.0 0.6 copy-start.8
  85.6 5.4 %collective-permute-start.6 = (bf16[8,5,216]{2,0,1:T(8,128)(2,1)}, bf16[8,5,216]{2,0,1:T(8,128)(2,1)}, u32[]{:S(2)}, u32[]{:S(2)}) collective-permute-start(bf16[8,5,216]{2,0,1:T(8,128)(2,1)} %get-tuple-element.22), channel_id=1, source_target_pairs={{0,1},{1,2},{2,3},{3,4},{4,5},{5,6},{6,7},{7,8},{8,9},{9,10},{10,1... | collective-permute-start | bytes 51848 | tf_op jit(solution)/shard_map/ppermute | solution.py:25
  90.2 4.0 %copy-start.4 = (bf16[32,216,216]{2,1,0:T(8,128)(2,1)S(1)}, bf16[32,216,216]{2,1,0:T(8,128)(2,1)}, u32[]{:S(2)}) copy-start(bf16[32,216,216]{2,1,0:T(8,128)(2,1)} %param.11) | copy-start | bytes 8957956
where the time goes:
time: 105 us; the launch traced here: 104 us
  starting transfers between devices  39.2 us (37%)
  other arithmetic  29.6 us (28%)
  local copies, waits for them, and re-layouts  15.5 us (15%)
  matrix products  12.6 us (12%)
  waiting for transfers between devices  4.27 us (4%)
  between operations  2.82 us (3%)
    ppermute x8, starting transfers between devices, from_behind(): return lax.ppermute(shard, axis, pairs)  24.4 us
    select_n x2, other arithmetic, place(): return jnp.where(live, window, jnp.zeros((), values.dtype))  11.6 us
    ppermute x2, starting transfers between devices, padded_2(): before = lax.ppermute(last, axis, up)  11 us
    dot_general x2, matrix products, run_sweeps(): jnp.einsum('enm,evm->evn', tiles_mass, rounded, preferred_element_type=jn...  5.56 us
    gather x2, local copies, waits for them, and re-layouts, run_sweeps(): beside = jnp.take(padded, near_index, axis=0, mode='clip')  5.32 us
    dot_general x2, matrix products, run_sweeps(): jnp.einsum('vh,ehn->evn', closure_out, hidden, preferred_element_type=jnp...  4.44 us
    ppermute x8, waiting for transfers between devices, from_behind(): return lax.ppermute(shard, axis, pairs)  4.26 us
    ppermute x2, starting transfers between devices, padded_2(): after = lax.ppermute(initial, axis, down)  3.84 us
  transfers between devices with their start and end apart: 12, of which 1 were waited for; matrix products, arithmetic and copies ran while one was open for 44% of the time, Pallas kernels for 0%

commit v1 on v0

v1 whole, which is shorter than its diff:
```python
import functools

import jax
import jax.numpy as jnp
from jax import lax
from jax.experimental import pallas as pl
from jax.experimental.pallas import tpu as pltpu
from jax.sharding import PartitionSpec as P

SUB = 8
LANE = 128
BF = jnp.bfloat16
F32 = jnp.float32

ANY = pl.BlockSpec(memory_space=pltpu.MemorySpace.HBM)
VM = pl.BlockSpec(memory_space=pltpu.VMEM)
SM = pl.BlockSpec(memory_space=pltpu.SMEM)
GROUP = 4


def cross_pairs(size):
    return [p for i in range(1, size - 1, 2) for p in ((i, i + 1), (i + 1, i))]


def intra_pairs(size):
    return [p for i in range(0, size - 1, 2) for p in ((i, i + 1), (i + 1, i))]


def swap_cross(x):
    return lax.ppermute(x, "dom", cross_pairs(lax.axis_size("dom")))


def swap_intra(x):
    return lax.ppermute(x, "dom", intra_pairs(lax.axis_size("dom")))


def lanes(shape):
    return lax.broadcasted_iota(jnp.int32, shape, len(shape) - 1)


def group_blocks(node):
    rem = node - LANE
    return GROUP + -(-GROUP * rem // LANE)


def pack_group(tile, put, node):
    rem = node - LANE
    rolled = []
    for k in range(GROUP):
        t = tile(k)
        put(k, t[:, :LANE])
        wide = jnp.concatenate(
            [t[:, LANE:].astype(F32), jnp.zeros((node, LANE - rem), F32)], axis=1
        )
        shift = k * rem % LANE
        rolled.append(pltpu.roll(wide, shift, 1) if shift else wide)
    lane = lanes((node, LANE))
    for b in range(group_blocks(node) - GROUP):
        block = None
        for k in range(GROUP):
            low, high = k * rem - b * LANE, (k + 1) * rem - b * LANE
            if high <= 0 or low >= LANE:
                continue
            block = rolled[k] if block is None else jnp.where(lane >= low, rolled[k], block)
        put(GROUP + b, block.astype(BF))


def unpack_group(block, put, node):
    rem = node - LANE
    lane = lanes((node, LANE))
    extra = [block(GROUP + b).astype(F32) for b in range(group_blocks(node) - GROUP)]
    for k in range(GROUP):
        first, last = k * rem // LANE, ((k + 1) * rem - 1) // LANE
        wide = extra[first]
        if last != first:
            wide = jnp.where(lane >= k * rem - first * LANE, wide, extra[last])
        shift = k * rem % LANE
        if shift:
            wide = pltpu.roll(wide, LANE - shift, 1)
        put(k, block(k), wide[:, :rem].astype(BF))


def tile_pass(values, wait, tiles, contract):
    nvar, count, node = values.shape
    rows = nvar * SUB
    member = lax.broadcasted_iota(jnp.int32, (rows, node), 0) % SUB
    outs = []
    for g in range(count // SUB):
        wait(g)
        part = values[:, g * SUB : (g + 1) * SUB, :].reshape(rows, node)
        acc = jnp.zeros((rows, node), F32)
        for k in range(SUB):
            lhs = jnp.where(member == k, part, 0.0).astype(BF)
            acc = acc + lax.dot_general(
                lhs,
                tiles[g * SUB + k],
                (((1,), (contract,)), ((), ())),
                preferred_element_type=F32,
            )
        outs.append(acc.reshape(nvar, SUB, node))
    return jnp.concatenate(outs, axis=1)


def spread_nets(cin, cout):
    hid, nvar = cin.shape

    def grow(matrix, rows, cols):
        left = (
            lax.broadcasted_iota(jnp.int32, (rows * SUB, rows), 0) // SUB
            == lax.broadcasted_iota(jnp.int32, (rows * SUB, rows), 1)
        ).astype(BF)
        right = (
            lax.broadcasted_iota(jnp.int32, (cols, cols * SUB), 1) // SUB
            == lax.broadcasted_iota(jnp.int32, (cols, cols * SUB), 0)
        ).astype(BF)
        tall = jnp.dot(left, matrix, preferred_element_type=F32).astype(BF)
        full = jnp.dot(tall, right, preferred_element_type=F32)
        shape = (rows * SUB, cols * SUB)
        same = (
            lax.broadcasted_iota(jnp.int32, shape, 0) % SUB
            == lax.broadcasted_iota(jnp.int32, shape, 1) % SUB
        )
        return jnp.where(same, full, 0.0).astype(BF)

    return grow(cin, hid, nvar), grow(cout, nvar, hid)


def closure_pass(values, net_in, net_out):
    nvar, count, node = values.shape
    outs = []
    for g in range(count // SUB):
        part = values[:, g * SUB : (g + 1) * SUB, :].reshape(nvar * SUB, node).astype(BF)
        hidden = jnp.tanh(jnp.dot(net_in, part, preferred_element_type=F32)).astype(BF)
        out = jnp.dot(net_out, hidden, preferred_element_type=F32)
        outs.append(out.reshape(nvar, SUB, node))
    return jnp.concatenate(outs, axis=1)


def couple(both, ext):
    half = both.shape[0] // 2
    out = jnp.dot(both, ext, preferred_element_type=F32)
    return out[:half] + out[half:]


def loader(src, dst, sems, step):
    count = src.shape[0] // step

    def copy(g):
        return pltpu.make_async_copy(
            src.at[pl.ds(g * step, step)], dst.at[pl.ds(g * step, step)], sems.at[g]
        )

    def start():
        for g in range(count):
            copy(g).start()

    return start, lambda g: copy(g).wait()


def pack_first(mass, out, tiles, sem, *, moving):
    node = mass.shape[1]
    parity = lax.axis_index("dom") % 2
    first = parity * (mass.shape[0] - moving)
    copy = pltpu.make_async_copy(mass.at[pl.ds(first, GROUP)], tiles, sem)
    copy.start()
    copy.wait()

    def put(b, value):
        out[b] = value

    pack_group(lambda k: tiles[k], put, node)


def pack_rest(mass, jac, mid, last, intra, tiles, own, sems, sends, *, moving):
    node, count = mass.shape[1], mass.shape[0]
    parity = lax.axis_index("dom") % 2
    first = parity * (count - moving)
    other = (1 - parity) * (count - moving)
    loads = [
        pltpu.make_async_copy(mass.at[pl.ds(first + GROUP, GROUP)], tiles.at[0], sems.at[0]),
        pltpu.make_async_copy(jac.at[pl.ds(first, GROUP)], tiles.at[1], sems.at[1]),
        pltpu.make_async_copy(jac.at[pl.ds(first + GROUP, GROUP)], tiles.at[2], sems.at[2]),
        pltpu.make_async_copy(mass.at[pl.ds(other, moving)], own.at[0], sems.at[3]),
        pltpu.make_async_copy(jac.at[pl.ds(other, moving)], own.at[1], sems.at[4]),
    ]
    for load in loads:
        load.start()
    blocks = group_blocks(node)
    for i in range(3):
        loads[i].wait()
        ref, base = (mid, i * blocks) if i < 2 else (last, 0)

        def put(b, value, ref=ref, base=base):
            ref[base + b] = value

        pack_group(lambda k, i=i: tiles[i, k], put, node)
        if i < 2:
            loads[3 + i].wait()
            pltpu.make_async_copy(
                own.at[i], intra.at[pl.ds(i * moving, moving)], sends.at[i]
            ).start()
    for i in range(2):
        pltpu.make_async_copy(
            own.at[i], intra.at[pl.ds(i * moving, moving)], sends.at[i]
        ).wait()


def column(row, count):
    shape = (count, count)
    same = lax.broadcasted_iota(jnp.int32, shape, 0) == lanes(shape)
    return jnp.sum(jnp.where(same, row, 0.0), axis=1, keepdims=True)


def store_sides(left, right, xout, iout):
    even = lax.axis_index("dom") % 2 == 0

    @pl.when(even)
    def _():
        for low, value in left:
            xout[low : low + value.shape[0], :] = value
        for low, value in right:
            iout[low : low + value.shape[0], :] = value

    @pl.when(jnp.logical_not(even))
    def _():
        for low, value in left:
            iout[low : low + value.shape[0], :] = value
        for low, value in right:
            xout[low : low + value.shape[0], :] = value


def first_mass(
    state, mass, near, penalty, order, owner,
    wout, both_out, keep_out, xout, iout,
    tiles, sems, *, reach,
):
    nvar, count, node = state.shape
    position = lax.axis_index("dom")
    start, wait = loader(mass, tiles, sems, SUB)
    start()
    faces = near.shape[0]
    found = near[...]
    located = jnp.where(found < 0, -1, found - (position * count - reach))
    pen = penalty[...].astype(F32)
    row = lax.broadcasted_iota(jnp.int32, (node, count), 0)
    col = lanes((node, count))
    matrix = jnp.zeros((node, count), F32)
    total = jnp.zeros((1, count), F32)
    for f in range(faces):
        matrix = matrix + jnp.where(row == located[f : f + 1], pen[f : f + 1], 0.0)
        total = total + pen[f : f + 1]
    matrix = matrix - jnp.where(row == col + reach, total, 0.0)
    matrix = matrix.T
    high = matrix.astype(BF)
    low = (matrix - high.astype(F32)).astype(BF)
    both_out[0:count, :] = high
    both_out[count : 2 * count, :] = low
    edge = order[...] + 1
    limit = column((edge * edge * edge).astype(F32), count)
    lane = lanes((count, node))
    keep_out[...] = (lane.astype(F32) < limit).astype(F32)
    goes = [column((owner[...] == position + d).astype(F32), count) for d in (-1, 1)]
    meta = [jnp.where(lane < LANE, limit, g).astype(BF) for g in goes]

    weighted = tile_pass(state[...].astype(F32), wait, tiles, 1).astype(BF)
    wout[...] = weighted
    sides = []
    for s, lo in enumerate((0, count - reach)):
        hi = lo + reach
        parts = [(v * reach, weighted[v, lo:hi, :]) for v in range(nvar)]
        base = nvar * reach
        parts += [(base, high[lo:hi]), (base + reach, low[lo:hi]), (base + 2 * reach, meta[s][lo:hi])]
        sides.append(parts)
    store_sides(sides[0], sides[1], xout, iout)


def first_rest(state, weighted, both, jac, cin, cout, part, nin, nout, tiles, sems, *, reach):
    nvar, count, node = state.shape
    start, wait = loader(jac, tiles, sems, SUB)
    start()
    net_in, net_out = spread_nets(cin[...], cout[...])
    nin[...] = net_in
    nout[...] = net_out
    values = state[...].astype(F32)
    local = weighted[...]
    pad = jnp.zeros((reach, node), BF)
    span = count + 2 * reach
    weights = both[:, :span]
    own = jnp.stack(
        [couple(weights, jnp.concatenate([pad, local[v], pad], axis=0)) for v in range(nvar)]
    )
    total = values + own + closure_pass(values, net_in, net_out)
    part[...] = total + tile_pass(local.astype(F32), wait, tiles, 0)


def take_sides(xin, iin, left, right):
    even = lax.axis_index("dom") % 2 == 0

    @pl.when(even)
    def _():
        left[...] = xin[...]
        right[...] = iin[...]

    @pl.when(jnp.logical_not(even))
    def _():
        left[...] = iin[...]
        right[...] = xin[...]


def halo_term(weights, left, right, nvar, reach, count, node):
    gap = jnp.zeros((count, node), BF)
    return jnp.stack(
        [
            couple(
                weights,
                jnp.concatenate(
                    [
                        left[v * reach : (v + 1) * reach, :],
                        gap,
                        right[v * reach : (v + 1) * reach, :],
                    ],
                    axis=0,
                ),
            )
            for v in range(nvar)
        ]
    )


def second(
    xin, iin, part, both, keep, nin, nout, mass, jac,
    wout, pout, xout, iout,
    mtiles, jtiles, left, right, msems, jsems, *, reach, moving,
):
    nvar, count, node = part.shape
    mstart, mwait = loader(mass, mtiles, msems, SUB)
    jstart, jwait = loader(jac, jtiles, jsems, SUB)
    mstart()
    jstart()
    take_sides(xin, iin, left, right)
    weights = both[:, : count + 2 * reach]
    current = part[...] + halo_term(weights, left, right, nvar, reach, count, node)
    current = current * keep[...][None]
    rounded = current.astype(BF).astype(F32)
    weighted = tile_pass(rounded, mwait, mtiles, 1).astype(BF)
    wout[...] = weighted
    pad = jnp.zeros((reach, node), BF)
    own = jnp.stack(
        [couple(weights, jnp.concatenate([pad, weighted[v], pad], axis=0)) for v in range(nvar)]
    )
    total = current + own + closure_pass(rounded, nin[...], nout[...])
    total = total + tile_pass(weighted.astype(F32), jwait, jtiles, 0)
    pout[...] = total
    sides = []
    for lo, edge in ((0, 0), (count - reach, count - moving)):
        parts = [(v * reach, weighted[v, lo : lo + reach, :]) for v in range(nvar)]
        near = total[:, edge : edge + moving, :].reshape(nvar * moving, node).astype(BF)
        parts.append((nvar * reach, near))
        sides.append(parts)
    store_sides(sides[0], sides[1], xout, iout)


def counts_of(owner, left, right, meta, reach):
    position = lax.axis_index("dom")
    below, kept = jnp.int32(0), jnp.int32(0)
    for e in range(owner.shape[0]):
        below = below + (owner[e] < position).astype(jnp.int32)
        kept = kept + (owner[e] == position).astype(jnp.int32)

    def taken(ref):
        flags = ref[meta : meta + reach, :].astype(F32)
        flags = jnp.where(lanes(flags.shape) == LANE, flags, 0.0)
        return jnp.sum(flags).astype(jnp.int32)

    return taken(left), below, kept, taken(right)


def place_own(
    xin1, iin1, owner, mass, jac,
    mout, jout, cnt_out,
    mtiles, jtiles, zero, left, right, msems, jsems, osems, zsems, *, reach, meta,
):
    count = mass.shape[0]
    slots = mout.shape[0]
    mstart, mwait = loader(mass, mtiles, msems, SUB)
    jstart, jwait = loader(jac, jtiles, jsems, SUB)
    mstart()
    jstart()
    take_sides(xin1, iin1, left, right)
    before, below, kept, after = counts_of(owner, left, right, meta, reach)
    cnt_out[0] = before
    cnt_out[1] = below
    cnt_out[2] = kept
    cnt_out[3] = after
    zero[...] = jnp.zeros_like(zero)
    filled = before + kept + after

    def blank(s):
        return (
            pltpu.make_async_copy(zero, mout.at[s], zsems.at[0, s]),
            pltpu.make_async_copy(zero, jout.at[s], zsems.at[1, s]),
        )

    def mass_copy(e):
        return pltpu.make_async_copy(mtiles.at[e], mout.at[before + e - below], osems.at[0, e])

    def jac_copy(e):
        return pltpu.make_async_copy(jtiles.at[e], jout.at[before + e - below], osems.at[1, e])

    def each(low, high, fun):
        lax.fori_loop(low, high, lambda i, c: (fun(i), c)[1], 0)

    def start_blank(s):
        for copy in blank(s):
            copy.start()

    def wait_all(copies):
        for copy in copies:
            copy.wait()

    each(filled, slots, start_blank)
    for g in range(count // SUB):
        mwait(g)
    each(below, below + kept, lambda e: mass_copy(e).start())
    for g in range(count // SUB):
        jwait(g)
    each(below, below + kept, lambda e: jac_copy(e).start())
    each(filled, slots, lambda s: wait_all(blank(s)))
    each(below, below + kept, lambda e: wait_all((mass_copy(e), jac_copy(e))))


def finish_state(
    xin1, iin1, xin2, iin2, part, weighted, both, keep, owner,
    out, left1, right1, left2, right2, joined, *, reach, moving, meta,
):
    nvar, count, node = part.shape
    slots = out.shape[1]
    take_sides(xin1, iin1, left1, right1)
    take_sides(xin2, iin2, left2, right2)
    before, below, kept, after = counts_of(owner, left1, right1, meta, reach)
    weights = both[:, : count + 2 * reach]
    span = count + 2 * reach
    current = part[...] + halo_term(weights, left2, right2, nvar, reach, count, node)
    joined[:, moving : moving + count, :] = current * keep[...][None]
    base = nvar * reach
    lane = lanes((moving, node)).astype(F32)
    blank = jnp.zeros((span - reach, node), BF)
    local = weighted[...]
    for ref1, ref2, pick, at, near in (
        (left1, left2, reach - moving, 0, 0),
        (right1, right2, 0, moving + count, 1),
    ):
        both_side = jnp.concatenate(
            [
                ref1[base : base + reach, :span].astype(F32)[pick : pick + moving],
                ref1[base + reach : base + 2 * reach, :span].astype(F32)[pick : pick + moving],
            ],
            axis=0,
        ).astype(BF)
        limit = ref1[meta : meta + reach, :LANE].astype(F32)[pick : pick + moving, 0:1]
        stay = (lane < limit).astype(F32)
        partial = ref2[base : base + nvar * moving, :].astype(F32)
        for v in range(nvar):
            if near == 0:
                ext = jnp.concatenate([blank, local[v, :reach, :]], axis=0)
            else:
                ext = jnp.concatenate([local[v, count - reach :, :], blank], axis=0)
            value = partial[v * moving : (v + 1) * moving] + couple(both_side, ext)
            joined[v, at : at + moving, :] = value * stay
    lead = moving - before + below
    filled = before + kept + after
    turn = lax.rem(slots - lead, slots)
    live = lax.broadcasted_iota(jnp.int32, (slots, node), 0) < filled
    for v in range(nvar):
        out[v] = jnp.where(live, pltpu.roll(joined[v], turn, 0), 0.0)


def place_early(cnt, c0, c1, intra, min_, jin, mout, jout, blocks, tiles, near, sems, osems, isems, *, moving):
    del min_, jin
    node = tiles.shape[2]
    size = group_blocks(node)
    even = lax.axis_index("dom") % 2 == 0
    loads = [
        pltpu.make_async_copy(c0, blocks.at[pl.ds(0, size)], sems.at[0]),
        pltpu.make_async_copy(c1, blocks.at[pl.ds(size, 2 * size)], sems.at[1]),
        pltpu.make_async_copy(intra, near, sems.at[2]),
    ]
    for load in loads:
        load.start()
    before, kept, after = cnt[0], cnt[2], cnt[3]
    left_slot, right_slot = before - moving, before + kept
    x_low = jnp.where(even, moving - before, 0)
    x_high = jnp.where(even, moving, after)
    x_slot = jnp.where(even, left_slot, right_slot)
    i_low = jnp.where(even, 0, moving - before)
    i_high = jnp.where(even, after, moving)
    i_slot = jnp.where(even, right_slot, left_slot)

    def each(low, high, fun):
        lax.fori_loop(low, high, lambda i, c: (fun(i), c)[1], 0)

    def from_near(k):
        return (
            pltpu.make_async_copy(near.at[k], mout.at[i_slot + k], isems.at[0, k]),
            pltpu.make_async_copy(near.at[moving + k], jout.at[i_slot + k], isems.at[1, k]),
        )

    def start_near(k):
        for copy in from_near(k):
            copy.start()

    def wait_near(k):
        for copy in from_near(k):
            copy.wait()

    loads[2].wait()
    each(i_low, i_high, start_near)

    def unpack(g):
        def put(k, main, rest):
            tiles[g * GROUP + k, :, :LANE] = main
            tiles[g * GROUP + k, :, LANE:] = rest

        unpack_group(lambda b: blocks[g * size + b], put, node)

    loads[0].wait()
    unpack(0)
    loads[1].wait()
    unpack(1)

    def mass_copy(k):
        return pltpu.make_async_copy(tiles.at[k], mout.at[x_slot + k], osems.at[k])

    each(x_low, x_high, lambda k: mass_copy(k).start())
    unpack(2)

    def jac_copy(k):
        return pltpu.make_async_copy(tiles.at[moving + k], jout.at[x_slot + k], osems.at[moving + k])

    top = jnp.minimum(x_high, GROUP)
    each(x_low, top, lambda k: jac_copy(k).start())
    each(i_low, i_high, wait_near)
    each(x_low, x_high, lambda k: mass_copy(k).wait())
    each(x_low, top, lambda k: jac_copy(k).wait())


def place_last(cnt, c2, jin, jout, tiles, osems, *, moving):
    del jin
    node = tiles.shape[2]
    even = lax.axis_index("dom") % 2 == 0
    before, kept, after = cnt[0], cnt[2], cnt[3]
    low = jnp.where(even, moving - before, 0)
    high = jnp.where(even, moving, after)
    slot = jnp.where(even, before - moving, before + kept)

    def put(k, main, rest):
        tiles[k, :, :LANE] = main
        tiles[k, :, LANE:] = rest

    unpack_group(lambda b: c2[b], put, node)

    def copy(k):
        return pltpu.make_async_copy(tiles.at[k - GROUP], jout.at[slot + k], osems.at[k])

    def each(fun):
        lax.fori_loop(jnp.maximum(low, GROUP), high, lambda i, c: (fun(i), c)[1], 0)

    each(lambda k: copy(k).start())
    each(lambda k: copy(k).wait())


def cost(flops, moved):
    return pl.CostEstimate(flops=flops, bytes_accessed=moved, transcendentals=0)


def call(kernel, outs, ins, specs, out_specs, scratch, aliases=None, moved=4_000_000):
    return pl.pallas_call(
        kernel,
        out_shape=outs,
        in_specs=specs,
        out_specs=out_specs,
        scratch_shapes=scratch,
        input_output_aliases=aliases or {},
        cost_estimate=cost(1_000_000, moved),
        compiler_params=pltpu.CompilerParams(vmem_limit_bytes=40 * 1024 * 1024),
    )(*ins)


def shards(
    elem_state, mass_inverse, jacobian, elem_order, new_owner, neighbors, penalty, closure_in, closure_out
):
    count, nvar, node = elem_state.shape
    hid = closure_in.shape[0]
    moving, reach = count // 4, count // 2
    slots = count + 2 * moving
    size = group_blocks(node)
    meta = nvar * reach + 2 * reach
    rows1 = meta + reach
    rows2 = nvar * (reach + moving)
    sds = jax.ShapeDtypeStruct
    dma = pltpu.SemaphoreType.DMA
    tile_buf = pltpu.VMEM((count, node, node), BF)
    gsems = dma((count // SUB,))

    state = jnp.transpose(elem_state, (1, 0, 2))
    near, pen = neighbors.T, penalty.T
    order, owner = elem_order[None, :], new_owner[None, :]

    c0 = call(
        functools.partial(pack_first, moving=moving),
        sds((size, node, LANE), BF), (mass_inverse,), [ANY], VM,
        [pltpu.VMEM((GROUP, node, node), BF), dma],
        moved=1_000_000,
    )
    r0 = swap_cross(c0)

    weighted, both, keep, x1, i1 = call(
        functools.partial(first_mass, reach=reach),
        (sds((nvar, count, node), BF), sds((2 * count, node), BF), sds((count, node), F32),
         sds((rows1, node), BF), sds((rows1, node), BF)),
        (state, mass_inverse, near, pen, order, owner),
        [VM, ANY, VM, VM, VM, VM], (VM,) * 5,
        [tile_buf, gsems],
    )
    rx1 = swap_cross(x1)
    ri1 = swap_intra(i1)

    c1, c2, ci = call(
        functools.partial(pack_rest, moving=moving),
        (sds((2 * size, node, LANE), BF), sds((size, node, LANE), BF), sds((2 * moving, node, node), BF)),
        (mass_inverse, jacobian), [ANY, ANY], (VM, VM, ANY),
        [pltpu.VMEM((3, GROUP, node, node), BF), pltpu.VMEM((2, moving, node, node), BF), dma((5,)), dma((2,))],
    )
    r1 = swap_cross(c1)
    rci = swap_intra(ci)

    part, nin, nout = call(
        functools.partial(first_rest, reach=reach),
        (sds((nvar, count, node), F32), sds((hid * SUB, nvar * SUB), BF), sds((nvar * SUB, hid * SUB), BF)),
        (state, weighted, both, jacobian, closure_in, closure_out),
        [VM, VM, VM, ANY, VM, VM], (VM, VM, VM),
        [tile_buf, gsems],
    )

    side1 = pltpu.VMEM((rows1, node), BF)
    side2 = pltpu.VMEM((rows2, node), BF)
    weighted2, part2, x2, i2 = call(
        functools.partial(second, reach=reach, moving=moving),
        (sds((nvar, count, node), BF), sds((nvar, count, node), F32),
         sds((rows2, node), BF), sds((rows2, node), BF)),
        (rx1, ri1, part, both, keep, nin, nout, mass_inverse, jacobian),
        [VM] * 7 + [ANY, ANY], (VM,) * 4,
        [tile_buf, tile_buf, side1, side1, gsems, gsems], moved=8_000_000,
    )
    rx2 = swap_cross(x2)
    ri2 = swap_intra(i2)
    r2 = swap_cross(c2)

    big = sds((slots, node, node), BF)
    mout, jout, cnt = call(
        functools.partial(place_own, reach=reach, meta=meta),
        (big, big, sds((4,), jnp.int32)),
        (rx1, ri1, new_owner, mass_inverse, jacobian),
        [VM, VM, SM, ANY, ANY], (ANY, ANY, SM),
        [tile_buf, tile_buf, pltpu.VMEM((node, node), BF), side1, side1, gsems, gsems,
         dma((2, count)), dma((2, slots))],
        moved=16_000_000,
    )
    final = call(
        functools.partial(finish_state, reach=reach, moving=moving, meta=meta),
        sds((nvar, slots, node), F32),
        (rx1, ri1, rx2, ri2, part2, weighted2, both, keep, new_owner),
        [VM] * 8 + [SM], VM,
        [side1, side1, side2, side2, pltpu.VMEM((nvar, slots, node), F32)],
        moved=2_000_000,
    )
    mout, jout = call(
        functools.partial(place_early, moving=moving),
        (big, big),
        (cnt, r0, r1, rci, mout, jout),
        [SM] + [ANY] * 5, (ANY, ANY),
        [pltpu.VMEM((3 * size, node, LANE), BF), pltpu.VMEM((3 * GROUP, node, node), BF),
         pltpu.VMEM((2 * moving, node, node), BF), dma((3,)), dma((2 * moving,)), dma((2, moving))],
        aliases={4: 0, 5: 1}, moved=6_000_000,
    )
    jout = call(
        functools.partial(place_last, moving=moving),
        big, (cnt, r2, jout), [SM, VM, ANY], ANY,
        [pltpu.VMEM((GROUP, node, node), BF), dma((moving,))],
        aliases={2: 0}, moved=1_000_000,
    )
    return jnp.transpose(final, (1, 0, 2)), mout, jout


def solution(mesh):
    placed = (
        P("dom", None, None),
        P("dom", None, None),
        P("dom", None, None),
        P("dom"),
        P("dom"),
        P("dom", None),
        P("dom", None),
        P(),
        P(),
    )

    return jax.shard_map(
        shards,
        mesh=mesh,
        in_specs=placed,
        out_specs=(P("dom", None, None), P("dom", None, None), P("dom", None, None)),
        check_vma=False,
    )
```

time: 105 us -> 92.6 us (0.88)
  Pallas kernels: 0 us -> 35.7 us
  other arithmetic: 29.6 us -> 0 us
  matrix products: 12.6 us -> 0 us
  starting transfers between devices: 39.2 us -> 33.5 us
  waiting for transfers between devices: 4.27 us -> 6.71 us
  between operations: 2.82 us -> 0.9 us
  local copies, waits for them, and re-layouts: 15.5 us -> 14.1 us
    pallas_call x0 -> x9, Pallas kernels: none -> 35.7 us  [call(): pl.pallas_call(kernel, out_shape=outs, in_specs=specs, out_specs=out_spec...]
    unnamed x26 -> x47, local copies, waits for them, and re-layouts: 0.66 us -> 14.1 us
    dot_general x6 -> x0, matrix products: 12.6 us -> none  [the longest x2 5.56 us: run_sweeps(): jnp.einsum('enm,evm->evn', tiles_mass, rounded, preferred_element_type=jn...]
    select_n x3 -> x0, other arithmetic: 11.7 us -> none  [the longest x2 11.6 us: place(): return jnp.where(live, window, jnp.zeros((), values.dtype))]
    slice x6 -> x0, local copies, waits for them, and re-layouts: 6.17 us -> none  [the longest x1 1.49 us: ship_owner(): return from_behind(new_owner[start_row:start_row + moving], 'dom', offset)]
    ppermute x12 -> x8, starting transfers between devices: 39.2 us -> 33.5 us  [the longest x5 18.6 us: swap_cross(): return lax.ppermute(x, 'dom', cross_pairs(lax.axis_size('dom')))]
    reduce_sum x3 -> x0, other arithmetic: 5.46 us -> none  [the longest x2 3.47 us: run_sweeps(): coupling = jnp.sum(weights_wide * difference, axis=1)]
    gather x2 -> x0, local copies, waits for them, and re-layouts: 5.32 us -> none  [run_sweeps(): beside = jnp.take(padded, near_index, axis=0, mode='clip')]
  transfers between devices with their start and end apart: 12 -> 8, of which waited for: 1 -> 2; matrix products, arithmetic and copies ran while one was open for 44% -> 1% of each run, Pallas kernels for 0% -> 33%
where the time goes in v1:
time: 92.6 us; the launch traced here: 91 us
  Pallas kernels  35.7 us (39%)
  starting transfers between devices  33.5 us (36%)
  local copies, waits for them, and re-layouts  14.1 us (15%)
  waiting for transfers between devices  6.71 us (7%)
    pallas_call x9, Pallas kernels, call(): pl.pallas_call(kernel, out_shape=outs, in_specs=specs, out_specs=out_spec...  35.7 us
    ppermute x5, starting transfers between devices, swap_cross(): return lax.ppermute(x, 'dom', cross_pairs(lax.axis_size('dom')))  18.6 us
    ppermute x3, starting transfers between devices, swap_intra(): return lax.ppermute(x, 'dom', intra_pairs(lax.axis_size('dom')))  14.9 us
    unnamed x47, local copies, waits for them, and re-layouts  14.1 us
    ppermute x5, waiting for transfers between devices, swap_cross(): return lax.ppermute(x, 'dom', cross_pairs(lax.axis_size('dom')))  6.7 us
  transfers between devices with their start and end apart: 8, of which 2 were waited for; matrix products, arithmetic and copies ran while one was open for 1% of the time, Pallas kernels for 33%

profile of v1, /device:TPU:7, one launch (start us, length us, event | category | flops | bytes accessed | tf_op | source)
XLA Modules:
  0.0 91.0 jit_solution(15324641302045810630)
XLA Ops:
  0.6 2.0 %copy-done = bf16[32,216,216]{2,1,0:T(8,128)(2,1)S(1)} copy-done((bf16[32,216,216]{2,1,0:T(8,128)(2,1)S(1)}, bf16[32,216,216]{2,1,0:T(8,128)(2,1)}, u32[]{:S(2)}) %copy-start) | copy-done | bytes 2986008
  2.6 2.0 %copy-done.2 = bf16[32,216,216]{2,1,0:T(8,128)(2,1)S(1)} copy-done((bf16[32,216,216]{2,1,0:T(8,128)(2,1)S(1)}, bf16[32,216,216]{2,1,0:T(8,128)(2,1)}, u32[]{:S(2)}) %copy-start.2) | copy-done | bytes 2986008
  4.7 3.6 %shard_map.118 = (bf16[14,216,128]{2,1,0:T(8,128)(2,1)}, bf16[7,216,128]{2,1,0:T(8,128)(2,1)}, bf16[16,216,216]{2,1,0:T(8,128)(2,1)}) custom-call(bf16[32,216,216]{2,1,0:T(8,128)(2,1)S(1)} %copy-done, bf16[32,216,216]{2,1,0:T(8,128)(2,1)S(1)} %copy-done.2), custom_call_target="tpu_custom_call" | custom-call | flops 1000000 | bytes 4000000 | tf_op jit(solution)/shard_map/pallas_call | solution.py:577
  8.2 0.7 collective-permute-start.6
  9.0 3.0 %collective-permute-start.5 = (bf16[14,216,128]{2,1,0:T(8,128)(2,1)}, bf16[14,216,128]{2,1,0:T(8,128)(2,1)}, u32[]{:S(2)}, u32[]{:S(2)}) collective-permute-start(bf16[14,216,128]{2,1,0:T(8,128)(2,1)} %get-tuple-element.36), channel_id=1, source_target_pairs={{1,2},{2,1},{3,4},{4,3},{5,6},{6,5},{7,8},{8,7},{9,10},{10,9},{11,... | collective-permute-start | bytes 2322440 | tf_op jit(solution)/shard_map/ppermute | solution.py:30
  12.0 1.2 %shard_map.117 = bf16[7,216,128]{2,1,0:T(8,128)(2,1)} custom-call(bf16[32,216,216]{2,1,0:T(8,128)(2,1)S(1)} %copy-done), custom_call_target="tpu_custom_call" | custom-call | flops 1000000 | bytes 1000000 | tf_op jit(solution)/shard_map/pallas_call | solution.py:577
  13.2 4.3 %collective-permute-start.4 = (bf16[7,216,128]{2,1,0:T(8,128)(2,1)}, bf16[7,216,128]{2,1,0:T(8,128)(2,1)}, u32[]{:S(2)}, u32[]{:S(2)}) collective-permute-start(bf16[7,216,128]{2,1,0:T(8,128)(2,1)} %shard_map.117), channel_id=1, source_target_pairs={{1,2},{2,1},{3,4},{4,3},{5,6},{6,5},{7,8},{8,7},{9,10},{10,9},{11,... | collective-permute-start | bytes 1161224 | tf_op jit(solution)/shard_map/ppermute | solution.py:30
  17.5 3.0 %collective-permute-start.7 = (bf16[7,216,128]{2,1,0:T(8,128)(2,1)}, bf16[7,216,128]{2,1,0:T(8,128)(2,1)}, u32[]{:S(2)}, u32[]{:S(2)}) collective-permute-start(bf16[7,216,128]{2,1,0:T(8,128)(2,1)} %get-tuple-element.41), channel_id=1, source_target_pairs={{1,2},{2,1},{3,4},{4,3},{5,6},{6,5},{7,8},{8,7},{9,10},{10,9},{11,... | collective-permute-start | bytes 1161224 | tf_op jit(solution)/shard_map/ppermute | solution.py:30
  20.6 3.9 %shard_map.112 = (bf16[5,32,216]{2,1,0:T(8,128)(2,1)S(1)}, bf16[64,216]{1,0:T(8,128)(2,1)S(1)}, f32[32,216]{1,0:T(8,128)S(1)}, bf16[128,216]{1,0:T(8,128)(2,1)S(1)}, bf16[128,216]{1,0:T(8,128)(2,1)}) custom-call(bf16[5,32,216]{2,1,0:T(8,128)(2,1)S(1)} %bitcast.6, bf16[32,216,216]{2,1,0:T(8,128)(2,1)S(1)} %copy-done.1, s32[6,32]{1,0:T(8,128)S(1)} %bitcast.9, ...), custom_call_target="tpu_custom_call" | custom-call | flops 1000000 | bytes 4000000 | tf_op jit(solution)/shard_map/pallas_call | solution.py:577
  24.6 0.6 copy-done.9
  25.2 0.6 copy-done.12
  25.8 0.6 copy-done.15
  26.4 4.3 %collective-permute-start = (bf16[128,216]{1,0:T(8,128)(2,1)S(1)}, bf16[128,216]{1,0:T(8,128)(2,1)S(1)}, u32[]{:S(2)}, u32[]{:S(2)}) collective-permute-start(bf16[128,216]{1,0:T(8,128)(2,1)S(1)} %get-tuple-element.23), channel_id=1, source_target_pairs={{1,2},{2,1},{3,4},{4,3},{5,6},{6,5},{7,8},{8,7},{9,10},{10,9},{11,... | collective-permute-start | bytes 165896 | tf_op jit(solution)/shard_map/ppermute | solution.py:30
  30.7 3.2 %collective-permute-done.xin.xin1 = bf16[128,216]{1,0:T(8,128)(2,1)S(1)} collective-permute-done((bf16[128,216]{1,0:T(8,128)(2,1)S(1)}, bf16[128,216]{1,0:T(8,128)(2,1)S(1)}, u32[]{:S(2)}, u32[]{:S(2)}) %collective-permute-start) | collective-permute-done | bytes 55328 | tf_op jit(solution)/shard_map/ppermute | solution.py:30
  33.9 0.6 copy-done.5
  34.5 14.2 %collective-permute-start.1 = (bf16[128,216]{1,0:T(8,128)(2,1)}, bf16[128,216]{1,0:T(8,128)(2,1)}, u32[]{:S(2)}, u32[]{:S(2)}) collective-permute-start(bf16[128,216]{1,0:T(8,128)(2,1)} %get-tuple-element.24), channel_id=1, source_target_pairs={{0,1},{1,0},{2,3},{3,2},{4,5},{5,4},{6,7},{7,6},{8,9},{9,8},{10,11... | collective-permute-start | bytes 165896 | tf_op jit(solution)/shard_map/ppermute | solution.py:34
  48.7 0.8 copy.15.cin
  49.5 2.0 %copy-done.3 = bf16[32,216,216]{2,1,0:T(8,128)(2,1)S(1)} copy-done((bf16[32,216,216]{2,1,0:T(8,128)(2,1)S(1)}, bf16[32,216,216]{2,1,0:T(8,128)(2,1)}, u32[]{:S(2)}) %copy-start.3) | copy-done | bytes 2986008
  51.5 0.9 copy-done.8
  52.4 0.8 copy-done.10
  53.1 0.9 copy-done.16
  54.0 0.7 copy-done.21
  54.7 3.8 %shard_map.113 = (f32[5,32,216]{2,1,0:T(8,128)S(1)}, bf16[512,40]{1,0:T(8,128)(2,1)S(1)}, bf16[40,512]{1,0:T(8,128)(2,1)S(1)}) custom-call(bf16[5,32,216]{2,1,0:T(8,128)(2,1)S(1)} %bitcast.7, bf16[5,32,216]{2,1,0:T(8,128)(2,1)S(1)} %copy-done.16, bf16[64,216]{1,0:T(8,128)(2,1)S(1)} %copy-done.10, bf16[32,216,216]{2,1,0:T(8,128)(2,1)S(1)} %copy-done.3, ...), custom_call_target="tpu_custom_call" | custom-call | flops 1000000 | bytes 4000000 | tf_op jit(solution)/shard_map/pallas_call | solution.py:577
  58.5 0.8 copy-done.6
  59.4 0.8 copy-done.13
  60.1 7.6 %shard_map.114 = (bf16[5,32,216]{2,1,0:T(8,128)(2,1)S(1)}, f32[5,32,216]{2,1,0:T(8,128)S(1)}, bf16[120,216]{1,0:T(8,128)(2,1)S(1)}, bf16[120,216]{1,0:T(8,128)(2,1)S(1)}) custom-call(bf16[128,216]{1,0:T(8,128)(2,1)S(1)} %copy-done.6, bf16[128,216]{1,0:T(8,128)(2,1)} %collective-permute-done.1.iin.iin1, f32[5,32,216]{2,1,0:T(8,128)S(1)} %get-tuple-element.27.part, ...), custom_call_target="tpu_custom_call" | custom-call | flops 1000000 | bytes 8000000 | tf_op jit(solution)/shard_map/pallas_call | solution.py:577
  67.8 3.9 %collective-permute-start.2 = (bf16[120,216]{1,0:T(8,128)(2,1)S(1)}, bf16[120,216]{1,0:T(8,128)(2,1)S(1)}, u32[]{:S(2)}, u32[]{:S(2)}) collective-permute-start(bf16[120,216]{1,0:T(8,128)(2,1)S(1)} %get-tuple-element.31), channel_id=1, source_target_pairs={{1,2},{2,1},{3,4},{4,3},{5,6},{6,5},{7,8},{8,7},{9,10},{10,9},{11,... | collective-permute-start | bytes 155528 | tf_op jit(solution)/shard_map/ppermute | solution.py:30
  71.7 3.5 %collective-permute-done.2.xin2 = bf16[120,216]{1,0:T(8,128)(2,1)S(1)} collective-permute-done((bf16[120,216]{1,0:T(8,128)(2,1)S(1)}, bf16[120,216]{1,0:T(8,128)(2,1)S(1)}, u32[]{:S(2)}, u32[]{:S(2)}) %collective-permute-start.2) | collective-permute-done | bytes 51872 | tf_op jit(solution)/shard_map/ppermute | solution.py:30
  75.3 7.8 %shard_map.116 = (bf16[48,216,216]{2,1,0:T(8,128)(2,1)}, bf16[48,216,216]{2,1,0:T(8,128)(2,1)}, s32[4]{0:T(128)S(1)}) custom-call(bf16[128,216]{1,0:T(8,128)(2,1)S(1)} %copy-done.6, bf16[128,216]{1,0:T(8,128)(2,1)} %collective-permute-done.1.iin.iin1, s32[32]{0:T(128)S(1)} %copy-done.18, bf16[32,216,216]{2,1,0:T(8,128)(2,1)S(1)} %copy-done.1, ...), custom_call_target="tpu_custom_call" | custom-call | flops 1000000 | bytes 16000000 | tf_op jit(solution)/shard_map/pallas_call | solution.py:577
  83.1 1.8 %shard_map.115 = f32[5,48,216]{2,1,0:T(8,128)} custom-call(bf16[128,216]{1,0:T(8,128)(2,1)S(1)} %copy-done.6, bf16[128,216]{1,0:T(8,128)(2,1)} %collective-permute-done.1.iin.iin1, bf16[120,216]{1,0:T(8,128)(2,1)S(1)} %collective-permute-done.2.xin2, bf16[120,216]{1,0:T(8,128)(2,1)S(1)} %collective-permute-done.3.iin2, ...), custom_call_target="tpu_custom_call" | custom-call | flops 1000000 | bytes 2000000 | tf_op jit(solution)/shard_map/pallas_call | solution.py:577
  85.0 4.1 %shard_map.119 = (bf16[48,216,216]{2,1,0:T(8,128)(2,1)}, bf16[48,216,216]{2,1,0:T(8,128)(2,1)}) custom-call(s32[4]{0:T(128)S(1)} %get-tuple-element.35.cnt, bf16[7,216,128]{2,1,0:T(8,128)(2,1)} %collective-permute-done.4.c0, bf16[14,216,128]{2,1,0:T(8,128)(2,1)} %collective-permute-done.5.c1, ...), custom_call_target="tpu_custom_call", output_to_operand_aliasing={{0}: (4, {}), {1}: (5, {})} | custom-call | flops 1000000 | bytes 6000000 | tf_op jit(solution)/shard_map/pallas_call | solution.py:577
  89.0 1.9 %shard_map.120 = bf16[48,216,216]{2,1,0:T(8,128)(2,1)} custom-call(s32[4]{0:T(128)S(1)} %get-tuple-element.35.cnt, bf16[7,216,128]{2,1,0:T(8,128)(2,1)} %collective-permute-done.7.c2, bf16[48,216,216]{2,1,0:T(8,128)(2,1)} %get-tuple-element.42.jin), custom_call_target="tpu_custom_call", output_to_operand_aliasing={{}: (2, {})} | custom-call | flops 1000000 | bytes 1000000 | tf_op jit(solution)/shard_map/pallas_call | solution.py:577
  (40 shorter events, 0.1 us)
Async XLA Ops:
  0.6 2.0 %copy-start = (bf16[32,216,216]{2,1,0:T(8,128)(2,1)S(1)}, bf16[32,216,216]{2,1,0:T(8,128)(2,1)}, u32[]{:S(2)}) copy-start(bf16[32,216,216]{2,1,0:T(8,128)(2,1)} %mass.9) | copy-start | bytes 8957956
  2.6 2.0 %copy-start.2 = (bf16[32,216,216]{2,1,0:T(8,128)(2,1)S(1)}, bf16[32,216,216]{2,1,0:T(8,128)(2,1)}, u32[]{:S(2)}) copy-start(bf16[32,216,216]{2,1,0:T(8,128)(2,1)} %jac.7) | copy-start | bytes 8957956
  4.6 15.9 %copy-start.1 = (bf16[32,216,216]{2,1,0:T(8,128)(2,1)S(1)}, bf16[32,216,216]{2,1,0:T(8,128)(2,1)}, u32[]{:S(2)}) copy-start(bf16[32,216,216]{2,1,0:T(8,128)(2,1)} %mass.9) | copy-start | bytes 8957956
  4.6 15.9 %copy-start.7 = (bf16[32,5,216]{2,0,1:T(8,128)(2,1)S(1)}, bf16[32,5,216]{2,0,1:T(8,128)(2,1)}, u32[]{:S(2)}) copy-start(bf16[32,5,216]{2,0,1:T(8,128)(2,1)} %param.9) | copy-start | bytes 207364
  4.6 15.9 %copy-start.17 = (s32[32]{0:T(128)S(1)}, s32[32]{0:T(128)}, u32[]{:S(2)}) copy-start(s32[32]{0:T(128)} %owner.3) | copy-start | bytes 388
  4.6 15.9 %copy-start.19 = (s32[32,6]{0,1:T(8,128)S(1)}, s32[32,6]{0,1:T(8,128)}, u32[]{:S(2)}) copy-start(s32[32,6]{0,1:T(8,128)} %param.14) | copy-start | bytes 2308
  4.6 15.9 %copy-start.20 = (bf16[32,6]{0,1:T(8,128)(2,1)S(1)}, bf16[32,6]{0,1:T(8,128)(2,1)}, u32[]{:S(2)}) copy-start(bf16[32,6]{0,1:T(8,128)(2,1)} %param.15) | copy-start | bytes 1156
  4.7 15.9 %copy-start.22 = (s32[32]{0:T(128)S(1)}, s32[32]{0:T(128)}, u32[]{:S(2)}) copy-start(s32[32]{0:T(128)} %param.12) | copy-start | bytes 388
  8.2 76.7 %collective-permute-start.6 = (bf16[16,216,216]{2,1,0:T(8,128)(2,1)}, bf16[16,216,216]{2,1,0:T(8,128)(2,1)}, u32[]{:S(2)}, u32[]{:S(2)}) collective-permute-start(bf16[16,216,216]{2,1,0:T(8,128)(2,1)} %get-tuple-element.37), channel_id=1, source_target_pairs={{0,1},{1,0},{2,3},{3,2},{4,5},{5,4},{6,7},{7,6},{8,9},{9,8},{10,11... | collective-permute-start | bytes 4478984 | tf_op jit(solution)/shard_map/ppermute | solution.py:34
  9.0 76.0 %collective-permute-start.5 = (bf16[14,216,128]{2,1,0:T(8,128)(2,1)}, bf16[14,216,128]{2,1,0:T(8,128)(2,1)}, u32[]{:S(2)}, u32[]{:S(2)}) collective-permute-start(bf16[14,216,128]{2,1,0:T(8,128)(2,1)} %get-tuple-element.36), channel_id=1, source_target_pairs={{1,2},{2,1},{3,4},{4,3},{5,6},{6,5},{7,8},{8,7},{9,10},{10,9},{11,... | collective-permute-start | bytes 2322440 | tf_op jit(solution)/shard_map/ppermute | solution.py:30
  13.2 71.8 %collective-permute-start.4 = (bf16[7,216,128]{2,1,0:T(8,128)(2,1)}, bf16[7,216,128]{2,1,0:T(8,128)(2,1)}, u32[]{:S(2)}, u32[]{:S(2)}) collective-permute-start(bf16[7,216,128]{2,1,0:T(8,128)(2,1)} %shard_map.117), channel_id=1, source_target_pairs={{1,2},{2,1},{3,4},{4,3},{5,6},{6,5},{7,8},{8,7},{9,10},{10,9},{11,... | collective-permute-start | bytes 1161224 | tf_op jit(solution)/shard_map/ppermute | solution.py:30
  17.5 71.5 %collective-permute-start.7 = (bf16[7,216,128]{2,1,0:T(8,128)(2,1)}, bf16[7,216,128]{2,1,0:T(8,128)(2,1)}, u32[]{:S(2)}, u32[]{:S(2)}) collective-permute-start(bf16[7,216,128]{2,1,0:T(8,128)(2,1)} %get-tuple-element.41), channel_id=1, source_target_pairs={{1,2},{2,1},{3,4},{4,3},{5,6},{6,5},{7,8},{8,7},{9,10},{10,9},{11,... | collective-permute-start | bytes 1161224 | tf_op jit(solution)/shard_map/ppermute | solution.py:30
  24.5 0.6 copy-start.9
  25.1 0.6 copy-start.12
  25.8 0.6 copy-start.15
  26.4 7.5 %collective-permute-start = (bf16[128,216]{1,0:T(8,128)(2,1)S(1)}, bf16[128,216]{1,0:T(8,128)(2,1)S(1)}, u32[]{:S(2)}, u32[]{:S(2)}) collective-permute-start(bf16[128,216]{1,0:T(8,128)(2,1)S(1)} %get-tuple-element.23), channel_id=1, source_target_pairs={{1,2},{2,1},{3,4},{4,3},{5,6},{6,5},{7,8},{8,7},{9,10},{10,9},{11,... | collective-permute-start | bytes 165896 | tf_op jit(solution)/shard_map/ppermute | solution.py:30
  33.9 0.6 copy-start.5
  34.5 24.0 %collective-permute-start.1 = (bf16[128,216]{1,0:T(8,128)(2,1)}, bf16[128,216]{1,0:T(8,128)(2,1)}, u32[]{:S(2)}, u32[]{:S(2)}) collective-permute-start(bf16[128,216]{1,0:T(8,128)(2,1)} %get-tuple-element.24), channel_id=1, source_target_pairs={{0,1},{1,0},{2,3},{3,2},{4,5},{5,4},{6,7},{7,6},{8,9},{9,8},{10,11... | collective-permute-start | bytes 165896 | tf_op jit(solution)/shard_map/ppermute | solution.py:34
  49.5 2.0 %copy-start.3 = (bf16[32,216,216]{2,1,0:T(8,128)(2,1)S(1)}, bf16[32,216,216]{2,1,0:T(8,128)(2,1)}, u32[]{:S(2)}) copy-start(bf16[32,216,216]{2,1,0:T(8,128)(2,1)} %jac.7) | copy-start | bytes 8957956
  51.5 0.9 copy-start.8
  52.4 0.8 copy-start.10
  53.1 0.9 copy-start.16
  54.0 0.7 copy-start.21
  54.7 3.8 %copy-start.4 = (bf16[32,216,216]{2,1,0:T(8,128)(2,1)S(1)}, bf16[32,216,216]{2,1,0:T(8,128)(2,1)}, u32[]{:S(2)}) copy-start(bf16[32,216,216]{2,1,0:T(8,128)(2,1)} %jac.7) | copy-start | bytes 8957956
  54.7 20.6 %copy-start.18 = (s32[32]{0:T(128)S(1)}, s32[32]{0:T(128)}, u32[]{:S(2)}) copy-start(s32[32]{0:T(128)} %owner.3) | copy-start | bytes 388
  58.5 0.8 copy-start.6
  59.4 0.8 copy-start.13
  67.8 15.3 %copy-start.11 = (bf16[64,216]{1,0:T(8,128)(2,1)S(1)}, bf16[64,216]{1,0:T(8,128)(2,1)}, u32[]{:S(2)}) copy-start(bf16[64,216]{1,0:T(8,128)(2,1)} %copy-done.9) | copy-start | bytes 82948
  67.8 15.3 %copy-start.14 = (f32[32,216]{1,0:T(8,128)S(1)}, f32[32,216]{1,0:T(8,128)}, u32[]{:S(2)}) copy-start(f32[32,216]{1,0:T(8,128)} %copy-done.12) | copy-start | bytes 82948
  67.8 7.5 %collective-permute-start.2 = (bf16[120,216]{1,0:T(8,128)(2,1)S(1)}, bf16[120,216]{1,0:T(8,128)(2,1)S(1)}, u32[]{:S(2)}, u32[]{:S(2)}) collective-permute-start(bf16[120,216]{1,0:T(8,128)(2,1)S(1)} %get-tuple-element.31), channel_id=1, source_target_pairs={{1,2},{2,1},{3,4},{4,3},{5,6},{6,5},{7,8},{8,7},{9,10},{10,9},{11,... | collective-permute-start | bytes 155528 | tf_op jit(solution)/shard_map/ppermute | solution.py:30
  75.3 7.8 %collective-permute-start.3 = (bf16[120,216]{1,0:T(8,128)(2,1)S(1)}, bf16[120,216]{1,0:T(8,128)(2,1)S(1)}, u32[]{:S(2)}, u32[]{:S(2)}) collective-permute-start(bf16[120,216]{1,0:T(8,128)(2,1)S(1)} %get-tuple-element.32), channel_id=1, source_target_pairs={{0,1},{1,0},{2,3},{3,2},{4,5},{5,4},{6,7},{7,6},{8,9},{9,8},{10,11... | collective-permute-start | bytes 155528 | tf_op jit(solution)/shard_map/ppermute | solution.py:34
